TPU v7x, 256 devices: a whole 4x4x8 slice. The times are simulated.
256 devices in a mesh: dp: 16 (over x, y), shard: 16 (over z, core).
Axes of the slice: x: 4, y: 4, z: 8, core: 2. Of those that a mesh axis runs over, the one named last changes fastest.
Arguments:
- gradient: bfloat16 [16, 4096, 6144], P('dp', None, 'shard'), may hold values from -400 to 400
- error_buffer: bfloat16 [16, 4096, 6144], P('dp', None, 'shard'), may hold values from -6 to 6
- right_init: float32 [6144, 32], P('shard'), may hold values from -6 to 6
- first_moment: float32 [4096, 6144], P(('dp', 'shard')), may hold values from -0.06 to 0.06
- second_moment: float32 [4096, 6144], P(('dp', 'shard')), may hold values from 0.001 to 0.01
Outputs:
- error_out: bfloat16 [16, 4096, 6144], P('dp', None, 'shard')
- first_out: float32 [4096, 6144], P(('dp', 'shard'))
- second_out: float32 [4096, 6144], P(('dp', 'shard'))
- direction: float32 [4096, 6144], P(('dp', 'shard'))
All inputs are finite; a program needn't handle non-finite values.
Results may differ from a plain program's by a relative error of at most 0.009.
Values sent between devices are 32-bit elements; how exact they have to be, the bound alone decides.
A program may use at most 64 MiB of HBM per device.

v0:
```python
import jax
import jax.numpy as jnp
from jax import lax
from jax.sharding import PartitionSpec as P

D = 4096
F = 6144
R = 32
CLIP_LEVEL = 0.9
BETA_ONE = 0.9
BETA_TWO = 0.95
EPSILON = 1e-08


def cut_along(x, dim, count):
    shape = x.shape
    tiles = x.reshape(*shape[:dim], count, shape[dim] // count, *shape[dim + 1 :])
    return jnp.moveaxis(tiles, dim, 0)


def sent_and_summed(x, axis, dim):
    tiles = cut_along(x, dim, lax.axis_size(axis))
    arrived = lax.all_to_all(tiles, axis, split_axis=0, concat_axis=0, tiled=True)
    return arrived.sum(axis=0)


def sent_to_all(x, axis):
    count = lax.axis_size(axis)
    return lax.all_to_all(jnp.broadcast_to(x[None], (count, *x.shape)), axis, 0, 0, tiled=True)


def taken_together(x, axis):
    return sent_to_all(x, axis).sum(axis=0)


def laid_out(tiles, dim):
    shape = list(tiles.shape[1:])
    shape[dim] *= tiles.shape[0]
    return jnp.moveaxis(tiles, 0, dim).reshape(shape)


def collect(x, axis, dim):
    return laid_out(sent_to_all(x, axis), dim)


def orthonormal(left_raw, gram_matrix):
    width = gram_matrix.shape[0]
    ridge_shift = 1e-06 * jnp.trace(gram_matrix) / width
    lower_factor = jnp.linalg.cholesky(
        gram_matrix + ridge_shift * jnp.eye(width, dtype=jnp.float32)
    )
    return lax.linalg.triangular_solve(
        lower_factor, left_raw, left_side=False, lower=True, transpose_a=True
    )


def local(gradient, error_buffer, right_init, first_moment, second_moment):
    replica_count = lax.axis_size("dp")
    shard_count = lax.axis_size("shard")
    merged = (gradient[0].astype(jnp.float32) + error_buffer[0].astype(jnp.float32)).astype(
        jnp.bfloat16
    )
    total_rows = merged.shape[0]
    left_part = jnp.dot(merged, right_init.astype(jnp.bfloat16), preferred_element_type=jnp.float32)
    row_share = sent_and_summed(left_part, "shard", 0)
    row_share = taken_together(row_share, "dp") / replica_count
    left_raw = lax.all_gather(row_share, "shard", axis=0, tiled=True)
    gram_matrix = jnp.dot(left_raw.T, left_raw, precision=lax.Precision.HIGHEST)
    left_orth = orthonormal(left_raw, gram_matrix)
    right_part = lax.dot_general(
        merged,
        left_orth.astype(jnp.bfloat16),
        (((0,), (0,)), ((), ())),
        preferred_element_type=jnp.float32,
    )
    right_mean = taken_together(right_part, "dp") / replica_count
    update = jnp.dot(left_orth, right_mean.T, precision=lax.Precision.HIGHEST)
    error_out = (merged.astype(jnp.float32) - update).astype(jnp.bfloat16)[None]
    slab_size = total_rows // replica_count
    own_count = slab_size // shard_count
    right_full = collect(right_mean, "shard", 0)
    first_row = (lax.axis_index("dp") * shard_count + lax.axis_index("shard")) * own_count
    left_own = lax.dynamic_slice_in_dim(left_orth, first_row, own_count, 0)
    owned_rows = jnp.dot(left_own, right_full.T, precision=lax.Precision.HIGHEST)
    square_total = jnp.sum(right_full * right_full)
    grad_norm = jnp.sqrt(square_total)
    clip_level = CLIP_LEVEL * jnp.sqrt(jnp.float32(R * (D + F)))
    scaled = owned_rows * (clip_level / jnp.maximum(grad_norm, clip_level))
    first_out = BETA_ONE * first_moment + (1.0 - BETA_ONE) * scaled
    second_out = BETA_TWO * second_moment + (1.0 - BETA_TWO) * scaled * scaled
    direction = first_out / (jnp.sqrt(second_out) + EPSILON)
    return (error_out, first_out, second_out, direction)


def solution(mesh):
    return jax.shard_map(
        local,
        mesh=mesh,
        in_specs=(
            P("dp", None, "shard"),
            P("dp", None, "shard"),
            P("shard", None),
            P(("dp", "shard"), None),
            P(("dp", "shard"), None),
        ),
        out_specs=(
            P("dp", None, "shard"),
            P(("dp", "shard"), None),
            P(("dp", "shard"), None),
            P(("dp", "shard"), None),
        ),
        check_vma=False,
    )
```

profile of v0, /device:TPU:1, one launch (start us, length us, event | category | flops | bytes accessed | tf_op | source)
XLA Modules:
  0.0 137.0 jit_solution(12787354762281012879)
XLA Ops:
  0.6 0.0 copy-start.2
  0.6 3.7 %add_convert_fusion = bf16[1,4096,384]{2,1,0:T(8,128)(2,1)S(1)} fusion(bf16[1,4096,384]{2,1,0:T(8,128)(2,1)} %param.6, bf16[1,4096,384]{2,1,0:T(8,128)(2,1)} %param.5), kind=kLoop, calls=%fused_computation.2 | loop fusion | flops 6291456 | bytes 9437184 | tf_op jit(solution)/shard_map/convert_element_type | solution.py:60
  4.3 0.0 copy-done.2
  4.3 1.1 fusion.5
  5.4 27.2 %all_to_all.20 = f32[16,256,32]{1,2,0:T(8,128)} all-to-all(f32[16,256,32]{1,2,0:T(8,128)S(1)} %fusion.5), channel_id=1, replica_groups=mesh['dp'=16,'shard'=16] {'shard'}, dimensions={0} | all-to-all | bytes 1048576 | tf_op jit(solution)/shard_map/all_to_all | solution.py:23
  32.6 1.1 reduce_sum.46
  33.7 18.0 %all_to_all.21 = f32[16,256,32]{1,2,0:T(8,128)} all-to-all(f32[16,256,32]{1,2,0:T(8,128)S(1)} %broadcast_in_dim.14), channel_id=1, replica_groups=mesh['dp'=16,'shard'=16] {'dp'}, dimensions={0} | all-to-all | bytes 1048576 | tf_op jit(solution)/shard_map/all_to_all | solution.py:29
  51.7 1.1 reduce_sum.47
  52.8 15.9 %all_gather.3 = f32[4096,32]{0,1:T(8,128)S(1)} all-gather(f32[256,32]{0,1:T(8,128)S(1)} %broadcast_multiply_fusion.1), channel_id=1, replica_groups=mesh['dp'=16,'shard'=16] {'shard'}, dimensions={0}, use_global_device_ids=true | all-gather | bytes 557056 | tf_op jit(solution)/shard_map/all_gather | solution.py:67
  68.7 0.0 copy-start
  68.7 0.8 copy-done
  69.5 1.2 select_reduce_fusion.1
  70.6 0.1 copy.14
  71.4 2.9 %cholesky.17 = f32[32,32]{1,0:T(8,128)S(1)} custom-call(f32[32,32]{1,0:T(8,128)S(1)} %fusion.12), custom_call_target="Cholesky" | custom-call | tf_op jit(solution)/shard_map/jit(cholesky)/cholesky | solution.py:49
  74.3 0.6 compare_reduce_fusion
  75.0 0.7 fusion.8
  75.6 2.4 %custom-call.6 = f32[1,32,32]{1,2,0:T(8,128)S(1)} custom-call(f32[1,32,32]{2,1,0:T(8,128)S(1)} %fusion.8), custom_call_target="InvertDiagBlocksLowerTriangular" | custom-call | tf_op jit(solution)/shard_map/triangular_solve | solution.py:52
  78.0 1.7 %fusion.9 = f32[4096,32]{0,1:T(8,128)S(1)} fusion(f32[4096,32]{0,1:T(8,128)} %copy-done, f32[1,32,32]{1,2,0:T(8,128)S(1)} %custom-call.6), kind=kOutput, calls=%fused_computation.18 | convolution fusion | flops 50331648 | bytes 1052672 | tf_op jit(solution)/shard_map/triangular_solve | solution.py:52
  79.7 0.0 copy-start.1
  79.7 0.8 copy-done.1
  80.6 0.5 fusion.1
  81.1 0.1 broadcast_in_dim.16
  81.2 16.7 %all_to_all.22 = f32[16,384,32]{1,2,0:T(8,128)} all-to-all(f32[16,384,32]{1,2,0:T(8,128)S(1)} %broadcast_in_dim.16), channel_id=1, replica_groups=mesh['dp'=16,'shard'=16] {'dp'}, dimensions={0} | all-to-all | bytes 1572864 | tf_op jit(solution)/shard_map/all_to_all | solution.py:29
  97.9 1.2 reduce_sum.49
  99.1 1.0 broadcast_in_dim.31
  100.1 7.3 %all-to-all-start.3 = ((f32[16,384,32]{1,2,0:T(8,128)}), f32[16,384,32]{1,2,0:T(8,128)}, u32[]{:S(2)}, u32[]{:S(2)}) async-start(f32[16,384,32]{1,2,0:T(8,128)} %broadcast_in_dim.31), calls=%async_computation.3 | async-start | bytes 1572864 | tf_op jit(solution)/shard_map/all_to_all | solution.py:29
  107.4 7.8 %fusion = bf16[1,4096,384]{2,1,0:T(8,128)(2,1)} fusion(f32[4096,32]{0,1:T(8,128)} %copy-done.1, bf16[1,4096,384]{2,1,0:T(8,128)(2,1)S(1)} %add_convert_fusion, f32[384,32]{0,1:T(8,128)S(1)} %reduce_sum.49), kind=kOutput, calls=%fused_computation.3 | convolution fusion | flops 608710656 | bytes 6864896 | tf_op jit(solution)/shard_map/dot_general | solution.py:77
  115.2 15.0 %all-to-all-done.3 = f32[16,384,32]{1,2,0:T(8,128)} async-done(((f32[16,384,32]{1,2,0:T(8,128)}), f32[16,384,32]{1,2,0:T(8,128)}, u32[]{:S(2)}, u32[]{:S(2)}) %all-to-all-start.3) | async-done | bytes 786464 | tf_op jit(solution)/shard_map/all_to_all | solution.py:29
  130.2 1.9 %multiply_reduce_fusion = f32[]{:T(128)} fusion(f32[16,384,32]{1,2,0:T(8,128)} %all-to-all-done.3), kind=kLoop, calls=%fused_computation.6 | loop fusion | flops 393215 | bytes 786436 | tf_op jit(solution)/shard_map/reduce_sum | solution.py:85
  132.9 1.2 copy.16
  134.1 3.0 %add_divide_fusion = (f32[16,6144]{1,0:T(8,128)}, f32[16,6144]{1,0:T(8,128)}, f32[16,6144]{1,0:T(8,128)}) fusion(f32[16,6144]{1,0:T(8,128)} %param.9, f32[16,6144]{1,0:T(8,128)} %param.8, f32[]{:T(128)S(6)} %div.36, f32[6144,32]{0,1:T(8,128)S(1)} %bitcast.30, f32[4096,32]{0,1:T(8,128)} %copy-done.1, s32[]{:T(128)S(6)} %select_n.14), kind=kOutput, calls=%fused_computation.9 | convolution fusion | flops 38731776 | bytes 2768904 | tf_op jit(solution)/shard_map/dot_general | solution.py:84
  (5 shorter events, 0.1 us)
Async XLA Ops:
  0.6 3.7 %copy-start.2 = (f32[384,32]{0,1:T(8,128)S(1)}, f32[384,32]{0,1:T(8,128)}, u32[]{:S(2)}) copy-start(f32[384,32]{0,1:T(8,128)} %param.7) | copy-start | bytes 147460
  68.7 0.8 copy-start
  79.7 0.8 copy-start.1
  100.1 30.1 %all-to-all-start.3 = ((f32[16,384,32]{1,2,0:T(8,128)}), f32[16,384,32]{1,2,0:T(8,128)}, u32[]{:S(2)}, u32[]{:S(2)}) async-start(f32[16,384,32]{1,2,0:T(8,128)} %broadcast_in_dim.31), calls=%async_computation.3 | async-start | bytes 1572864 | tf_op jit(solution)/shard_map/all_to_all | solution.py:29
where the time goes:
time: 138 us; the launch traced here: 137 us
  blocking collectives  77.8 us (56%)
  other arithmetic  15.6 us (11%)
  matrix products  15.2 us (11%)
  waiting for transfers between devices  15 us (11%)
  starting transfers between devices  7.33 us (5%)
  local copies, waits for them, and re-layouts  3.97 us (3%)
  between operations  2.13 us (2%)
    all_to_all x2, blocking collectives, sent_to_all(): lax.all_to_all(jnp.broadcast_to(x[None], (count, *x.shape)), axis, 0, 0,...  34.7 us
    all_to_all x1, blocking collectives, sent_and_summed(): lax.all_to_all(tiles, axis, split_axis=0, concat_axis=0, tiled=True)  27.2 us
    all_gather x1, blocking collectives, local(): left_raw = lax.all_gather(row_share, 'shard', axis=0, tiled=True)  15.9 us
    all_to_all x1, waiting for transfers between devices, sent_to_all(): lax.all_to_all(jnp.broadcast_to(x[None], (count, *x.shape)), axis, 0, 0,...  15 us
    dot_general x1, matrix products, local(): update = jnp.dot(left_orth, right_mean.T, precision=lax.Precision.HIGHEST)  7.79 us
    all_to_all x1, starting transfers between devices, sent_to_all(): lax.all_to_all(jnp.broadcast_to(x[None], (count, *x.shape)), axis, 0, 0,...  7.33 us
    convert_element_type x1, other arithmetic, local(): (gradient[0].astype(jnp.float32) + error_buffer[0].astype(jnp.float32)).a...  3.66 us
    another operation x3, other arithmetic, orthonormal(): jnp.linalg.cholesky(gram_matrix + ridge_shift * jnp.eye(width, dtype=jnp....  3.59 us
  transfers between devices with their start and end apart: 1, of which 1 were waited for; matrix products, arithmetic and copies ran while one was open for 6% of the time, Pallas kernels for 0%

commit v1 on v0

--- a/solution.py
+++ b/solution.py
@@ -64,7 +64,9 @@
     left_part = jnp.dot(merged, right_init.astype(jnp.bfloat16), preferred_element_type=jnp.float32)
     row_share = sent_and_summed(left_part, "shard", 0)
     row_share = taken_together(row_share, "dp") / replica_count
-    left_raw = lax.all_gather(row_share, "shard", axis=0, tiled=True)
+    left_raw = jnp.concatenate(
+        lax.all_to_all(jnp.stack([row_share] * lax.axis_size("shard")), "shard", 0, 0), axis=0
+    )
     gram_matrix = jnp.dot(left_raw.T, left_raw, precision=lax.Precision.HIGHEST)
     left_orth = orthonormal(left_raw, gram_matrix)
     right_part = lax.dot_general(

time: 138 us -> 139 us (level)
  blocking collectives: 77.8 us -> 82.9 us
  starting transfers between devices: 7.33 us -> 4.18 us
    all_to_all x0 -> x1, blocking collectives: none -> 20.8 us  [local(): lax.all_to_all(jnp.stack([row_share] * lax.axis_size('shard')), 'shard',...]
    all_gather x1 -> x0, blocking collectives: 15.9 us -> none  [local(): left_raw = lax.all_gather(row_share, 'shard', axis=0, tiled=True)]
    all_to_all x1, starting transfers between devices: 7.33 us -> 4.18 us  [sent_to_all(): lax.all_to_all(jnp.broadcast_to(x[None], (count, *x.shape)), axis, 0, 0,...]
where the time goes in v1:
time: 139 us
  blocking collectives  82.9 us (60%)
  other arithmetic  15.6 us (11%)
  waiting for transfers between devices  14.6 us (11%)
  matrix products  14.1 us (10%)
  local copies, waits for them, and re-layouts  5.11 us (4%)
  starting transfers between devices  4.18 us (3%)
  between operations  2.16 us (2%)
    all_to_all x2, blocking collectives, sent_to_all(): lax.all_to_all(jnp.broadcast_to(x[None], (count, *x.shape)), axis, 0, 0,...  35 us
    all_to_all x1, blocking collectives, sent_and_summed(): lax.all_to_all(tiles, axis, split_axis=0, concat_axis=0, tiled=True)  27.2 us
    all_to_all x1, blocking collectives, local(): lax.all_to_all(jnp.stack([row_share] * lax.axis_size('shard')), 'shard',...  20.8 us
    all_to_all x1, waiting for transfers between devices, sent_to_all(): lax.all_to_all(jnp.broadcast_to(x[None], (count, *x.shape)), axis, 0, 0,...  14.6 us
    dot_general x1, matrix products, local(): update = jnp.dot(left_orth, right_mean.T, precision=lax.Precision.HIGHEST)  7.8 us
    all_to_all x1, starting transfers between devices, sent_to_all(): lax.all_to_all(jnp.broadcast_to(x[None], (count, *x.shape)), axis, 0, 0,...  4.18 us
    convert_element_type x1, other arithmetic, local(): (gradient[0].astype(jnp.float32) + error_buffer[0].astype(jnp.float32)).a...  3.66 us
    another operation x3, other arithmetic, orthonormal(): jnp.linalg.cholesky(gram_matrix + ridge_shift * jnp.eye(width, dtype=jnp....  3.59 us
  transfers between devices with their start and end apart: 1, of which 1 were waited for; matrix products, arithmetic and copies ran while one was open for 6% of the time, Pallas kernels for 0%

profile of v1, /device:TPU:1, one launch (start us, length us, event | category | flops | bytes accessed | tf_op | source)
XLA Modules:
  0.0 138.8 jit_solution(14257257940599692220)
XLA Ops:
  0.6 0.0 copy-start.2
  0.6 3.7 %add_convert_fusion = bf16[1,4096,384]{2,1,0:T(8,128)(2,1)S(1)} fusion(bf16[1,4096,384]{2,1,0:T(8,128)(2,1)} %param.6, bf16[1,4096,384]{2,1,0:T(8,128)(2,1)} %param.5), kind=kLoop, calls=%fused_computation.2 | loop fusion | flops 6291456 | bytes 9437184 | tf_op jit(solution)/shard_map/convert_element_type | solution.py:60
  4.3 0.0 copy-done.2
  4.3 1.1 fusion.5
  5.4 27.2 %all_to_all.25 = f32[16,256,32]{1,2,0:T(8,128)} all-to-all(f32[16,256,32]{1,2,0:T(8,128)S(1)} %fusion.5), channel_id=1, replica_groups=mesh['dp'=16,'shard'=16] {'shard'}, dimensions={0} | all-to-all | bytes 1048576 | tf_op jit(solution)/shard_map/all_to_all | solution.py:23
  32.6 1.1 reduce_sum.46
  33.7 18.0 %all_to_all.26 = f32[16,256,32]{1,2,0:T(8,128)} all-to-all(f32[16,256,32]{1,2,0:T(8,128)S(1)} %broadcast_in_dim.14), channel_id=1, replica_groups=mesh['dp'=16,'shard'=16] {'dp'}, dimensions={0} | all-to-all | bytes 1048576 | tf_op jit(solution)/shard_map/all_to_all | solution.py:29
  51.7 1.1 reduce_sum.47
  52.8 20.8 %all_to_all.27 = f32[16,256,32]{1,2,0:T(8,128)S(1)} all-to-all(f32[16,256,32]{1,2,0:T(8,128)S(1)} %stack.2), channel_id=1, replica_groups=mesh['dp'=16,'shard'=16] {'shard'}, dimensions={0} | all-to-all | bytes 1048576 | tf_op jit(solution)/shard_map/all_to_all | solution.py:68
  73.6 0.0 copy-start
  73.6 0.8 copy-done
  74.4 1.2 select_reduce_fusion.1
  75.5 0.1 copy.17
  76.3 2.9 %cholesky.17 = f32[32,32]{1,0:T(8,128)S(1)} custom-call(f32[32,32]{1,0:T(8,128)S(1)} %fusion.12), custom_call_target="Cholesky" | custom-call | tf_op jit(solution)/shard_map/jit(cholesky)/cholesky | solution.py:49
  79.2 0.6 compare_reduce_fusion
  79.9 0.7 fusion.8
  80.5 2.4 %custom-call.6 = f32[1,32,32]{1,2,0:T(8,128)S(1)} custom-call(f32[1,32,32]{2,1,0:T(8,128)S(1)} %fusion.8), custom_call_target="InvertDiagBlocksLowerTriangular" | custom-call | tf_op jit(solution)/shard_map/triangular_solve | solution.py:52
  83.0 1.1 copy.19
  84.1 0.6 fusion.9
  84.7 0.0 copy-start.1
  84.7 0.8 copy-done.1
  85.5 0.5 fusion.1
  86.0 0.1 broadcast_in_dim.16
  86.1 17.0 %all_to_all.28 = f32[16,384,32]{1,2,0:T(8,128)} all-to-all(f32[16,384,32]{1,2,0:T(8,128)S(1)} %broadcast_in_dim.16), channel_id=1, replica_groups=mesh['dp'=16,'shard'=16] {'dp'}, dimensions={0} | all-to-all | bytes 1572864 | tf_op jit(solution)/shard_map/all_to_all | solution.py:29
  103.1 1.2 reduce_sum.49
  104.3 1.0 broadcast_in_dim.31
  105.3 4.2 %all-to-all-start.4 = ((f32[16,384,32]{1,2,0:T(8,128)}), f32[16,384,32]{1,2,0:T(8,128)}, u32[]{:S(2)}, u32[]{:S(2)}) async-start(f32[16,384,32]{1,2,0:T(8,128)} %broadcast_in_dim.31), calls=%async_computation.4 | async-start | bytes 1572864 | tf_op jit(solution)/shard_map/all_to_all | solution.py:29
  109.5 7.8 %fusion = bf16[1,4096,384]{2,1,0:T(8,128)(2,1)} fusion(f32[4096,32]{0,1:T(8,128)} %copy-done.1, bf16[1,4096,384]{2,1,0:T(8,128)(2,1)S(1)} %add_convert_fusion, f32[384,32]{0,1:T(8,128)S(1)} %reduce_sum.49), kind=kOutput, calls=%fused_computation.3 | convolution fusion | flops 608710656 | bytes 6864896 | tf_op jit(solution)/shard_map/dot_general | solution.py:79
  117.3 14.6 %all-to-all-done.4 = f32[16,384,32]{1,2,0:T(8,128)} async-done(((f32[16,384,32]{1,2,0:T(8,128)}), f32[16,384,32]{1,2,0:T(8,128)}, u32[]{:S(2)}, u32[]{:S(2)}) %all-to-all-start.4) | async-done | bytes 786464 | tf_op jit(solution)/shard_map/all_to_all | solution.py:29
  132.0 1.9 %multiply_reduce_fusion = f32[]{:T(128)} fusion(f32[16,384,32]{1,2,0:T(8,128)} %all-to-all-done.4), kind=kLoop, calls=%fused_computation.7 | loop fusion | flops 393215 | bytes 786436 | tf_op jit(solution)/shard_map/reduce_sum | solution.py:87
  134.6 1.2 copy.20
  135.8 3.0 %add_divide_fusion = (f32[16,6144]{1,0:T(8,128)}, f32[16,6144]{1,0:T(8,128)}, f32[16,6144]{1,0:T(8,128)}) fusion(f32[16,6144]{1,0:T(8,128)} %param.9, f32[16,6144]{1,0:T(8,128)} %param.8, f32[]{:T(128)S(6)} %div.36, f32[6144,32]{0,1:T(8,128)S(1)} %bitcast.35, f32[4096,32]{0,1:T(8,128)} %copy-done.1, s32[]{:T(128)S(6)} %select_n.14), kind=kOutput, calls=%fused_computation.10 | convolution fusion | flops 38731776 | bytes 2768904 | tf_op jit(solution)/shard_map/dot_general | solution.py:86
  (6 shorter events, 0.1 us)
Async XLA Ops:
  0.6 3.7 %copy-start.2 = (f32[384,32]{0,1:T(8,128)S(1)}, f32[384,32]{0,1:T(8,128)}, u32[]{:S(2)}) copy-start(f32[384,32]{0,1:T(8,128)} %param.7) | copy-start | bytes 147460
  73.6 0.8 copy-start
  84.7 0.8 copy-start.1
  105.3 26.6 %all-to-all-start.4 = ((f32[16,384,32]{1,2,0:T(8,128)}), f32[16,384,32]{1,2,0:T(8,128)}, u32[]{:S(2)}, u32[]{:S(2)}) async-start(f32[16,384,32]{1,2,0:T(8,128)} %broadcast_in_dim.31), calls=%async_computation.4 | async-start | bytes 1572864 | tf_op jit(solution)/shard_map/all_to_all | solution.py:29
